TPU v7x, 32 devices: a whole 2x2x4 slice. The times are simulated.
32 devices in a mesh: gx: 8 (over z, x), gy: 4 (over y, core).
Axes of the slice: x: 2, y: 2, z: 4, core: 2. Of those that a mesh axis runs over, the one named last changes fastest.
Arguments:
- right_side: float32 [128, 128, 128], P('gx', 'gy'), may hold values from -13 to 13
- accumulation: float32 [128, 128, 128], P('gx', 'gy'), may hold values from 0.05 to 0.5
- trans_x: float32 [128, 128, 128], P('gx', 'gy'), may hold values from 0.1 to 2
- trans_y: float32 [128, 128, 128], P('gx', 'gy'), may hold values from 0.1 to 2
- trans_z: float32 [128, 128, 128], P('gx', 'gy'), may hold values from 0.1 to 2
- perf_cells: int32 [512, 256], P(('gx', 'gy')), may hold values from 0 to 65535
- perf_live: int32 [512, 256], P(('gx', 'gy')), may hold values 0 or 1
- well_region: int32 [512, 1], P(('gx', 'gy')), may hold values from 0 to 7; in each aligned block of 16 rows (0 to 15, 16 to 31, ...) at most 2 rows name the same one
- schur_blocks: float32 [512, 256, 256], P(('gx', 'gy')), may hold values from -8 to 10, as said below
Outputs:
- pressure_update: float32 [128, 128, 128], P('gx', 'gy')
- residual: float32 [128, 128, 128], P('gx', 'gy')
Inputs may be any that keep to these rules, and one draw needn't show every extreme that they name: `perf_cells`: well w is owned by the device at position w // 16 of gx+gy; its slot's cell is a flat index (x slowest, layer fastest) within the block of 16 x 32 x 128 cells of the device at x index well_region[w] and at the owner's y index. `well_region`: among the wells of one owner, no x index is named more than 2 times, and some x index exactly 2 times. `schur_blocks`: each block is symmetric positive definite.
All inputs are finite; a program needn't handle non-finite values. No bound on the sum of `perf_live` on one device may be relied on, other than what follows from the above.
Results may differ from a plain program's by a relative error of at most 0.0003.
Values sent between devices are 32-bit elements; how exact they have to be, the bound alone decides.
A program may use at most 64 MiB of HBM per device.

v0:
```python
import functools

import jax
import jax.numpy as jnp
from jax import lax
from jax.experimental import pallas as pl
from jax.experimental.pallas import tpu as pltpu
from jax.sharding import PartitionSpec as P

WCAP = 2
ITERS = 6
GROUPS = (6, 8)
EARLY = 6
MESH = pl.DeviceIdType.MESH


def split_bf16(values):
    high = values.astype(jnp.bfloat16).astype(jnp.float32)
    return high, values - high


def kernel(
    n,
    ny,
    rows_x,
    rows_y,
    region_ref,
    rhs_hbm,
    acc_hbm,
    tx_hbm,
    ty_hbm,
    tz_hbm,
    cells_ref,
    live_ref,
    schur_hbm,
    x_ref,
    r_ref,
    rhs_ref,
    acc_ref,
    tx_ref,
    ty_ref,
    tz_ref,
    schur_vm,
    schur_two,
    onehot,
    vl_ref,
    lay_ref,
    live_slot,
    req_send,
    req_recv,
    send_b,
    recv_b,
    send_c,
    recv_c,
    send_g,
    recv_g,
    ysend,
    xrecv,
    yrecv,
    yface_send,
    xface_recv,
    yface_recv,
    fx_ref,
    fy_ref,
    py_ref,
    fz_ref,
    pz_ref,
    inv_ref,
    m_ref,
    w_ref,
    z_ref,
    p_ref,
    s_ref,
    nloc_ref,
    dots_ref,
    local_sem,
    field_sem,
    req_ss,
    req_rs,
    face_ss,
    face_rs,
    halo_ss,
    halo_rs,
    b_ss,
    b_rs,
    c_ss,
    c_rs,
    g_ss,
    g_rs,
):
    cols, layers = rhs_ref.shape
    wells, perf = cells_ref.shape
    chunk = WCAP * perf
    shift = layers.bit_length() - 1
    assert layers == 1 << shift and n == 1 << (n.bit_length() - 1)
    me, my = lax.axis_index("gx"), lax.axis_index("gy")

    def across(d):
        peer = me
        for bit in range(n.bit_length() - 1):
            if d >> bit & 1:
                peer = peer + (1 << bit) * (1 - 2 * lax.rem(lax.div(me, 1 << bit), 2))
        return peer

    def at_peer(d):
        return {"gx": across(d)}

    def at_x(d):
        return {"gx": lax.rem(me + (d + n), n)}

    def at_y(d):
        return {"gy": lax.rem(my + (d + ny), ny)}

    def remote(src, dst, ss, rs, where):
        return pltpu.make_async_remote_copy(
            src_ref=src, dst_ref=dst, send_sem=ss, recv_sem=rs, device_id=where, device_id_type=MESH
        )

    schur_copy = pltpu.make_async_copy(schur_hbm, schur_vm, local_sem)
    loads = [
        pltpu.make_async_copy(src, dst, field_sem.at[i])
        for i, (src, dst) in enumerate(
            (
                (ty_hbm, ty_ref),
                (tx_hbm, tx_ref),
                (tz_hbm, tz_ref),
                (acc_hbm, acc_ref),
                (rhs_hbm, rhs_ref),
            )
        )
    ]
    for copy in loads:
        copy.start()
    schur_copy.start()
    xrecv[...] = jnp.zeros_like(xrecv)
    barrier = pltpu.get_barrier_semaphore()
    for d in range(1, n):
        pl.semaphore_signal(barrier, inc=1, device_id=at_peer(d), device_id_type=MESH)
    for d in range(1, ny):
        pl.semaphore_signal(barrier, inc=1, device_id=at_y(d), device_id_type=MESH)

    well_at = []
    for d in range(n):
        peer = across(d)
        found = [jnp.int32(0)] * WCAP
        count = jnp.int32(0)
        for w in range(wells):
            match = region_ref[0, w] == peer
            for j in range(WCAP):
                found[j] = jnp.where(jnp.logical_and(match, count == j), jnp.int32(w), found[j])
            count = count + match.astype(jnp.int32)
        well_at.append(found)
        target = req_send if d else req_recv
        for j in range(WCAP):
            used = (count > j).astype(jnp.int32)
            span = slice(j * perf, (j + 1) * perf)
            target[d, :, span] = cells_ref[pl.ds(found[j], 1), :] * used
            live_slot[d, :, span] = (live_ref[pl.ds(found[j], 1), :] * used).astype(jnp.float32)
    loads[0].wait()
    loads[1].wait()
    yface_send[...] = ty_ref[pl.ds(rows_y - 1, rows_x, stride=rows_y), :]

    pl.semaphore_wait(barrier, n - 1 + ny - 1)
    requests = [
        remote(req_send.at[d], req_recv.at[d], req_ss.at[d], req_rs.at[d], at_peer(d)) for d in range(1, n)
    ]
    face_out = [
        remote(
            tx_ref.at[pl.ds(cols - rows_y, rows_y)], xface_recv, face_ss.at[0], face_rs.at[0], at_x(1)
        ),
        remote(yface_send, yface_recv, face_ss.at[1], face_rs.at[1], at_y(1)),
    ]
    for copy in requests[::-1] + face_out:
        copy.start()

    schur_copy.wait()
    for d in range(n):
        for j in range(WCAP):
            slot = d * WCAP + j
            block = schur_vm[well_at[d][j]]
            high = block.astype(jnp.bfloat16)
            schur_two[slot, 0:perf, :] = high
            schur_two[slot, perf : 2 * perf, :] = (block - high.astype(jnp.float32)).astype(jnp.bfloat16)

    last_x = me == n - 1
    last_y = my == ny - 1
    lane = lax.broadcasted_iota(jnp.int32, (rows_y, layers), 1)
    row = lax.broadcasted_iota(jnp.int32, (rows_y, layers), 0)
    zeros = jnp.zeros((rows_y, layers), jnp.float32)
    for copy in loads[2:]:
        copy.wait()
    for copy in face_out:
        copy.wait()
    fx_ref[0:rows_y, :] = jnp.where(me == 0, 0.0, xface_recv[...])
    for i in range(rows_x):
        at = slice(i * rows_y, (i + 1) * rows_y)
        after = slice((i + 1) * rows_y, (i + 2) * rows_y)
        fx = tx_ref[at, :]
        if i == rows_x - 1:
            fx = jnp.where(last_x, 0.0, fx)
        fx_ref[after, :] = fx
        fy = ty_ref[at, :]
        below = jnp.where(my == 0, 0.0, yface_recv[i : i + 1, :])
        py = jnp.where(row == 0, below, pltpu.roll(fy, 1, 0))
        fy = jnp.where(jnp.logical_and(last_y, row == rows_y - 1), 0.0, fy)
        fy_ref[at, :] = fy
        py_ref[at, :] = py
        fz = jnp.where(lane == layers - 1, 0.0, tz_ref[at, :])
        pz = pltpu.roll(fz, 1, 1)
        fz_ref[at, :] = fz
        pz_ref[at, :] = pz
        diagonal = acc_ref[at, :] + fx + fx_ref[at, :] + fy + py + fz + pz
        inverse = 1.0 / diagonal
        inv_ref[at, :] = inverse
        r = rhs_ref[at, :]
        r_ref[at, :] = r
        u = r * inverse
        m_ref[at, :] = u
        for ref in (x_ref, w_ref, z_ref, p_ref, s_ref):
            ref[at, :] = zeros
    dots_ref[...] = jnp.zeros_like(dots_ref)

    column = lax.broadcasted_iota(jnp.int32, (cols, chunk), 0)
    for d in range(n):
        if d:
            requests[d - 1].wait_recv()
        cells = req_recv[d]
        lay_ref[d] = jnp.bitwise_and(cells, layers - 1)
        onehot[:, d * chunk : (d + 1) * chunk] = (
            (column == lax.shift_right_logical(cells, shift)).astype(jnp.float32).astype(jnp.bfloat16)
        )
    for copy in requests:
        copy.wait_send()

    layer = lax.broadcasted_iota(jnp.int32, (layers, chunk), 0)
    pick_row = lax.broadcasted_iota(jnp.int32, (16, perf), 0)

    half = layers // 2
    first_half = lax.broadcasted_iota(jnp.int32, (1, layers), 1) < half

    def b_copy(par, d):
        return remote(send_b.at[par, d], recv_b.at[par, d], b_ss.at[par, d], b_rs.at[par, d], at_peer(d))

    def c_copy(par, d):
        return remote(send_c.at[par, d], recv_c.at[par, d], c_ss.at[par, d], c_rs.at[par, d], at_peer(d))

    def g_copy(par, d, slot):
        return remote(send_g.at[par], recv_g.at[par, slot], g_ss.at[par, d], g_rs.at[par, slot], at_y(d))

    def halo_copies(par):
        return [
            remote(
                m_ref.at[pl.ds(cols - rows_y, rows_y)],
                xrecv.at[par, 0],
                halo_ss.at[par, 0],
                halo_rs.at[par, 0],
                at_x(1),
            ),
            remote(
                m_ref.at[pl.ds(0, rows_y)], xrecv.at[par, 1], halo_ss.at[par, 1], halo_rs.at[par, 1], at_x(-1)
            ),
            remote(ysend.at[par, 0], yrecv.at[par, 0], halo_ss.at[par, 2], halo_rs.at[par, 2], at_y(1)),
            remote(ysend.at[par, 1], yrecv.at[par, 1], halo_ss.at[par, 3], halo_rs.at[par, 3], at_y(-1)),
        ]

    def start_sums(par):
        total = recv_b[par, 0, :, chunk:]
        for d in range(1, n):
            total = total + recv_b[par, d, :, chunk:]
        send_g[par] = total
        for d in range(1, ny):
            g_copy(par, d, ny - d).start()
        return total

    def end_sums(par, total):
        for d in range(1, ny):
            g_copy(par, d, d).wait_recv()
            total = total + recv_g[par, d]
        for d in range(1, ny):
            g_copy(par, d, d).wait_send()
        gam = jnp.sum(jnp.where(first_half, total, 0.0), axis=1, keepdims=True)
        dlt = jnp.sum(jnp.where(first_half, 0.0, total), axis=1, keepdims=True)
        return jnp.broadcast_to(gam, (1, layers)), jnp.broadcast_to(dlt, (1, layers))

    def step(k, carried):
        gam_old, a_old = carried
        par = lax.rem(k, 2)
        ysend[par, 0] = m_ref[pl.ds(rows_y - 1, rows_x, stride=rows_y), :]
        ysend[par, 1] = m_ref[pl.ds(0, rows_x, stride=rows_y), :]
        halos = halo_copies(par)
        x_up, x_down = halos[:2]
        pl.when(me < n - 1)(x_up.start)
        pl.when(me > 0)(x_down.start)
        for copy in halos[2:]:
            copy.start()

        turned = m_ref[...].T
        high, low = split_bf16(turned)
        lhs = jnp.concatenate([high, low], 0).astype(jnp.bfloat16)
        dots = dots_ref[...]
        for d in range(n - 1, -1, -1):
            part = jnp.dot(
                lhs, onehot[:, d * chunk : (d + 1) * chunk], preferred_element_type=jnp.float32
            )
            part = part[:layers] + part[layers:]
            picked = jnp.sum(jnp.where(layer == lay_ref[d], part, 0.0), axis=0, keepdims=True)
            target = send_b if d else recv_b
            target[par, d, :, :chunk] = picked
            target[par, d, :, chunk:] = dots
            if d:
                b_copy(par, d).start()

        def push(d):
            if d:
                b_copy(par, d).wait_recv()
            target = send_c if d else recv_c
            for j in range(WCAP):
                span = slice(j * perf, (j + 1) * perf)
                live = live_slot[d, :, span]
                high, low = split_bf16(recv_b[par, d, :, span] * live)
                left = jnp.where(pick_row == 0, high, jnp.where(pick_row == 1, low, 0.0)).astype(jnp.bfloat16)
                pushed = jnp.dot(
                    jnp.concatenate([left, left], 1),
                    schur_two[d * WCAP + j],
                    preferred_element_type=jnp.float32,
                )
                target[par, d, :, span] = jnp.sum(pushed, axis=0, keepdims=True) * live
            if d:
                c_copy(par, d).start()

        for d in range(EARLY):
            push(d)
        @pl.when(me < n - 1)
        def _():
            x_up.wait_send()
            x_down.wait_recv()

        @pl.when(me > 0)
        def _():
            x_up.wait_recv()
            x_down.wait_send()

        for copy in halos[2:]:
            copy.wait()
        for i in range(rows_x):
            at = slice(i * rows_y, (i + 1) * rows_y)
            after = slice((i + 1) * rows_y, (i + 2) * rows_y)
            m = m_ref[at, :]
            below = m_ref[(i - 1) * rows_y : i * rows_y, :] if i else xrecv[par, 0]
            above = m_ref[after, :] if i < rows_x - 1 else xrecv[par, 1]
            y_prev = jnp.where(row == 0, yrecv[par, 0, i : i + 1, :], pltpu.roll(m, 1, 0))
            y_next = jnp.where(row == rows_y - 1, yrecv[par, 1, i : i + 1, :], pltpu.roll(m, rows_y - 1, 0))
            nloc_ref[at, :] = (
                acc_ref[at, :] * m
                + fx_ref[after, :] * (m - above)
                + fx_ref[at, :] * (m - below)
                + fy_ref[at, :] * (m - y_next)
                + py_ref[at, :] * (m - y_prev)
                + fz_ref[at, :] * (m - pltpu.roll(m, layers - 1, 1))
                + pz_ref[at, :] * (m - pltpu.roll(m, 1, 1))
            )
        for d in range(EARLY, n):
            push(d)
        total = start_sums(par)
        gam, dlt = end_sums(par, total)
        b = jnp.where(k <= 1, 0.0, gam / gam_old)
        a = jnp.where(k == 0, 0.0, jnp.where(k == 1, gam / dlt, gam / (dlt - b * gam / a_old)))
        a_w = jnp.where(k == 0, -1.0, a)
        gamma = jnp.zeros((8, layers), jnp.float32)
        for i in range(rows_x):
            at = slice(i * rows_y, (i + 1) * rows_y)
            inverse = inv_ref[at, :]
            r = r_ref[at, :]
            p = r * inverse + b * p_ref[at, :]
            s = w_ref[at, :] + b * s_ref[at, :]
            p_ref[at, :] = p
            s_ref[at, :] = s
            x_ref[at, :] = x_ref[at, :] + a * p
            r = r - a * s
            r_ref[at, :] = r
            gamma = gamma + jnp.sum((r * r * inverse).reshape(rows_y // 8, 8, layers), axis=0)

        ends = [n * part // 8 for part in GROUPS]
        for first, end in zip([0] + ends[:-1], ends):
            for d in range(first, end):
                if d:
                    c_copy(par, d).wait_recv()
                high, low = split_bf16(recv_c[par, d])
                here = layer == lay_ref[d]
                span = slice(d * chunk, (d + 1) * chunk)
                vl_ref[0:layers, span] = jnp.where(here, high, 0.0).astype(jnp.bfloat16)
                vl_ref[layers : 2 * layers, span] = jnp.where(here, low, 0.0).astype(jnp.bfloat16)
            span = slice(first * chunk, end * chunk)
            wide = lax.dot_general(
                onehot[:, span],
                vl_ref[:, span],
                (((1,), (1,)), ((), ())),
                preferred_element_type=jnp.float32,
            )
            if end < n:
                nloc_ref[...] += wide[:, :layers] + wide[:, layers:]
        delta = jnp.zeros((8, layers), jnp.float32)
        for i in range(rows_x):
            at = slice(i * rows_y, (i + 1) * rows_y)
            z = nloc_ref[at, :] + (wide[at, :layers] + wide[at, layers:]) + b * z_ref[at, :]
            z_ref[at, :] = z
            w = w_ref[at, :] - a_w * z
            w_ref[at, :] = w
            m = w * inv_ref[at, :]
            m_ref[at, :] = m
            delta = delta + jnp.sum((m * r_ref[at, :]).reshape(rows_y // 8, 8, layers), axis=0)
        gamma = jnp.sum(gamma, axis=0, keepdims=True)
        delta = jnp.sum(delta, axis=0, keepdims=True)
        dots_ref[...] = jnp.where(
            first_half, gamma + pltpu.roll(gamma, half, 1), delta + pltpu.roll(delta, half, 1)
        )
        for d in range(1, n):
            b_copy(par, d).wait_send()
            c_copy(par, d).wait_send()
        return gam, a

    ones = jnp.ones((1, layers), jnp.float32)
    gam_old, a_old = lax.fori_loop(0, ITERS, step, (ones, ones))

    par = ITERS % 2
    recv_b[par, 0, :, chunk:] = dots_ref[...]
    for d in range(n - 1, 0, -1):
        send_b[par, d, :, chunk:] = dots_ref[...]
        b_copy(par, d).start()
    for d in range(1, n):
        b_copy(par, d).wait_recv()
    total = start_sums(par)
    for d in range(1, n):
        b_copy(par, d).wait_send()
    gam, dlt = end_sums(par, total)
    b = gam / gam_old
    a = gam / (dlt - b * gam / a_old)
    for i in range(rows_x):
        at = slice(i * rows_y, (i + 1) * rows_y)
        r = r_ref[at, :]
        p = r * inv_ref[at, :] + b * p_ref[at, :]
        s = w_ref[at, :] + b * s_ref[at, :]
        x_ref[at, :] = x_ref[at, :] + a * p
        r_ref[at, :] = r - a * s


def hand_on(x_ref, r_ref, x_out, r_out):
    x_out[...] = x_ref[...]
    r_out[...] = r_ref[...]


def local(
    right_side,
    accumulation,
    trans_x,
    trans_y,
    trans_z,
    perf_cells,
    perf_live,
    well_region,
    schur_blocks,
):
    rows_x, rows_y, layers = right_side.shape
    cols = rows_x * rows_y
    wells, perf = perf_cells.shape
    n, ny = lax.axis_size("gx"), lax.axis_size("gy")
    chunk = WCAP * perf
    f32, bf16, i32 = jnp.float32, jnp.bfloat16, jnp.int32
    vmem, dma = pltpu.VMEM, pltpu.SemaphoreType.DMA
    field = vmem((cols, layers), f32)
    fields = [value.reshape(cols, layers) for value in (right_side, accumulation, trans_x, trans_y, trans_z)]
    in_vmem = pl.BlockSpec(memory_space=pltpu.VMEM)
    outs = pl.pallas_call(
        functools.partial(kernel, n, ny, rows_x, rows_y),
        out_shape=[jax.ShapeDtypeStruct((cols, layers), f32)] * 2,
        in_specs=[pl.BlockSpec(memory_space=pltpu.SMEM)]
        + [pl.BlockSpec(memory_space=pl.ANY)] * 5
        + [in_vmem] * 2
        + [pl.BlockSpec(memory_space=pl.ANY)],
        out_specs=[in_vmem] * 2,
        scratch_shapes=[field] * 5
        + [
            vmem((wells, perf, perf), f32),
            vmem((n * WCAP, 2 * perf, perf), bf16),
            vmem((cols, n * chunk), bf16),
            vmem((2 * layers, n * chunk), bf16),
            vmem((n, 1, chunk), i32),
            vmem((n, 1, chunk), f32),
            vmem((n, 1, chunk), i32),
            vmem((n, 1, chunk), i32),
            vmem((2, n, 1, chunk + layers), f32),
            vmem((2, n, 1, chunk + layers), f32),
            vmem((2, n, 1, chunk), f32),
            vmem((2, n, 1, chunk), f32),
            vmem((2, 1, layers), f32),
            vmem((2, ny, 1, layers), f32),
            vmem((2, 2, rows_x, layers), f32),
            vmem((2, 2, rows_y, layers), f32),
            vmem((2, 2, rows_x, layers), f32),
            vmem((rows_x, layers), f32),
            vmem((rows_y, layers), f32),
            vmem((rows_x, layers), f32),
            vmem((cols + rows_y, layers), f32),
        ]
        + [field] * 11
        + [
            vmem((1, layers), f32),
            dma,
            dma((5,)),
            dma((n,)),
            dma((n,)),
            dma((2,)),
            dma((2,)),
            dma((2, 4)),
            dma((2, 4)),
            dma((2, n)),
            dma((2, n)),
            dma((2, n)),
            dma((2, n)),
            dma((2, ny)),
            dma((2, ny)),
        ],
        compiler_params=pltpu.CompilerParams(
            collective_id=0, has_side_effects=True, vmem_limit_bytes=60 * 1024 * 1024
        ),
    )(well_region.reshape(1, wells), *fields, perf_cells, perf_live, schur_blocks)
    outs = pl.pallas_call(
        hand_on,
        out_shape=[jax.ShapeDtypeStruct((cols, layers), f32)] * 2,
        in_specs=[in_vmem] * 2,
        out_specs=[in_vmem] * 2,
    )(*outs)
    return tuple(value.reshape(right_side.shape) for value in outs)


def solution(mesh):
    field, rows = P("gx", "gy", None), P(("gx", "gy"), None)
    return jax.shard_map(
        local,
        mesh=mesh,
        in_specs=(field,) * 5 + (rows,) * 3 + (P(("gx", "gy"), None, None),),
        out_specs=(field, field),
        check_vma=False,
    )
```

profile of v0, /device:TPU:0, one launch (start us, length us, event | category | flops | bytes accessed | tf_op | source)
XLA Modules:
  0.0 92.1 jit_solution(17672296786531447436)
XLA Ops:
  0.6 89.6 %shard_map.104 = (f32[512,128]{1,0:T(8,128)}, f32[512,128]{1,0:T(8,128)}) custom-call(s32[1,16]{1,0:T(1,128)} %bitcast.13, f32[512,128]{1,0:T(8,128)} %bitcast.8, f32[512,128]{1,0:T(8,128)} %bitcast.9, f32[512,128]{1,0:T(8,128)} %bitcast.10, f32[512,128]{1,0:T(8,128)} %bitcast.11, f32[512,128]{1,0:T(8,128)} %bitcast.12, s32[16,256]{1,0:T(8,128)} %cells_ref.1, ...), custom_call_target="tpu_custom_call" | custom-call | tf_op jit(solution)/shard_map/pallas_call | solution.py:473
  90.2 1.8 %shard_map.105 = (f32[512,128]{1,0:T(8,128)}, f32[512,128]{1,0:T(8,128)}) custom-call(f32[512,128]{1,0:T(8,128)} %get-tuple-element.6.x_ref, f32[512,128]{1,0:T(8,128)} %get-tuple-element.7.r_ref), custom_call_target="tpu_custom_call" | custom-call | tf_op jit(solution)/shard_map/pallas_call | solution.py:527
where the time goes:
time: 92.3 us; the launch traced here: 92.1 us
  Pallas kernels  91.4 us (99%)
    pallas_call x1, Pallas kernels, local(): pl.pallas_call(functools.partial(kernel, n, ny, rows_x, rows_y), out_shap...  89.6 us

commit v1 on v0

--- a/solution.py
+++ b/solution.py
@@ -9,8 +9,6 @@
 
 WCAP = 2
 ITERS = 6
-GROUPS = (6, 8)
-EARLY = 6
 MESH = pl.DeviceIdType.MESH
 
 
@@ -41,11 +39,12 @@
     ty_ref,
     tz_ref,
     schur_vm,
+    schur_out,
+    schur_in,
     schur_two,
     onehot,
     vl_ref,
     lay_ref,
-    live_slot,
     req_send,
     req_recv,
     send_b,
@@ -75,6 +74,8 @@
     dots_ref,
     local_sem,
     field_sem,
+    schur_ss,
+    schur_rs,
     req_ss,
     req_rs,
     face_ss,
@@ -110,6 +111,12 @@
 
     def at_y(d):
         return {"gy": lax.rem(my + (d + ny), ny)}
+
+    def at_other():
+        return {"gy": my + 1 - 2 * lax.rem(my, 2)}
+
+    def at_cross(d):
+        return {"gx": across(d), **at_other()}
 
     def remote(src, dst, ss, rs, where):
         return pltpu.make_async_remote_copy(
@@ -138,6 +145,8 @@
         pl.semaphore_signal(barrier, inc=1, device_id=at_peer(d), device_id_type=MESH)
     for d in range(1, ny):
         pl.semaphore_signal(barrier, inc=1, device_id=at_y(d), device_id_type=MESH)
+    for d in range(1, n):
+        pl.semaphore_signal(barrier, inc=1, device_id=at_cross(d), device_id_type=MESH)
 
     well_at = []
     for d in range(n):
@@ -154,13 +163,13 @@
         for j in range(WCAP):
             used = (count > j).astype(jnp.int32)
             span = slice(j * perf, (j + 1) * perf)
-            target[d, :, span] = cells_ref[pl.ds(found[j], 1), :] * used
-            live_slot[d, :, span] = (live_ref[pl.ds(found[j], 1), :] * used).astype(jnp.float32)
+            open_slot = live_ref[pl.ds(found[j], 1), :] * used
+            target[d, :, span] = (cells_ref[pl.ds(found[j], 1), :] + 1) * open_slot - 1
     loads[0].wait()
     loads[1].wait()
     yface_send[...] = ty_ref[pl.ds(rows_y - 1, rows_x, stride=rows_y), :]
 
-    pl.semaphore_wait(barrier, n - 1 + ny - 1)
+    pl.semaphore_wait(barrier, 2 * (n - 1) + ny - 1)
     requests = [
         remote(req_send.at[d], req_recv.at[d], req_ss.at[d], req_rs.at[d], at_peer(d)) for d in range(1, n)
     ]
@@ -173,14 +182,27 @@
     for copy in requests[::-1] + face_out:
         copy.start()
 
+    edges = [n, n - 1]
+    while edges[-1] > 3:
+        edges.append(edges[-1] - 2)
+    edges.append(0)
+    ranges = [range(low, high) for high, low in zip(edges[:-1], edges[1:])]
+    swaps = [
+        remote(
+            schur_out.at[pl.ds(d * WCAP, WCAP)],
+            schur_in.at[pl.ds(d * WCAP, WCAP)],
+            schur_ss.at[d],
+            schur_rs.at[d],
+            at_other(),
+        )
+        for d in range(n)
+    ]
     schur_copy.wait()
-    for d in range(n):
-        for j in range(WCAP):
-            slot = d * WCAP + j
-            block = schur_vm[well_at[d][j]]
-            high = block.astype(jnp.bfloat16)
-            schur_two[slot, 0:perf, :] = high
-            schur_two[slot, perf : 2 * perf, :] = (block - high.astype(jnp.float32)).astype(jnp.bfloat16)
+    for group in ranges:
+        for d in group:
+            for j in range(WCAP):
+                schur_out[d * WCAP + j] = schur_vm[well_at[d][j]]
+            swaps[d].start()
 
     last_x = me == n - 1
     last_y = my == ny - 1
@@ -239,10 +261,10 @@
     first_half = lax.broadcasted_iota(jnp.int32, (1, layers), 1) < half
 
     def b_copy(par, d):
-        return remote(send_b.at[par, d], recv_b.at[par, d], b_ss.at[par, d], b_rs.at[par, d], at_peer(d))
+        return remote(send_b.at[par, d], recv_b.at[par, d], b_ss.at[par, d], b_rs.at[par, d], at_cross(d))
 
     def c_copy(par, d):
-        return remote(send_c.at[par, d], recv_c.at[par, d], c_ss.at[par, d], c_rs.at[par, d], at_peer(d))
+        return remote(send_c.at[par, d], recv_c.at[par, d], c_ss.at[par, d], c_rs.at[par, d], at_cross(d))
 
     def g_copy(par, d, slot):
         return remote(send_g.at[par], recv_g.at[par, slot], g_ss.at[par, d], g_rs.at[par, slot], at_y(d))
@@ -282,54 +304,37 @@
         dlt = jnp.sum(jnp.where(first_half, 0.0, total), axis=1, keepdims=True)
         return jnp.broadcast_to(gam, (1, layers)), jnp.broadcast_to(dlt, (1, layers))
 
-    def step(k, carried):
-        gam_old, a_old = carried
-        par = lax.rem(k, 2)
+    def start_halos(par):
         ysend[par, 0] = m_ref[pl.ds(rows_y - 1, rows_x, stride=rows_y), :]
         ysend[par, 1] = m_ref[pl.ds(0, rows_x, stride=rows_y), :]
         halos = halo_copies(par)
-        x_up, x_down = halos[:2]
-        pl.when(me < n - 1)(x_up.start)
-        pl.when(me > 0)(x_down.start)
+        pl.when(me < n - 1)(halos[0].start)
+        pl.when(me > 0)(halos[1].start)
         for copy in halos[2:]:
             copy.start()
 
-        turned = m_ref[...].T
-        high, low = split_bf16(turned)
+    def send_field(par):
+        high, low = split_bf16(m_ref[...].T)
         lhs = jnp.concatenate([high, low], 0).astype(jnp.bfloat16)
         dots = dots_ref[...]
-        for d in range(n - 1, -1, -1):
-            part = jnp.dot(
-                lhs, onehot[:, d * chunk : (d + 1) * chunk], preferred_element_type=jnp.float32
-            )
-            part = part[:layers] + part[layers:]
-            picked = jnp.sum(jnp.where(layer == lay_ref[d], part, 0.0), axis=0, keepdims=True)
-            target = send_b if d else recv_b
-            target[par, d, :, :chunk] = picked
-            target[par, d, :, chunk:] = dots
-            if d:
+        for group in ranges:
+            for d in group:
+                part = jnp.dot(
+                    lhs, onehot[:, d * chunk : (d + 1) * chunk], preferred_element_type=jnp.float32
+                )
+                part = part[:layers] + part[layers:]
+                picked = jnp.sum(jnp.where(layer == lay_ref[d], part, 0.0), axis=0, keepdims=True)
+                send_b[par, d, :, :chunk] = picked
+                send_b[par, d, :, chunk:] = dots
+            for d in group:
                 b_copy(par, d).start()
-
-        def push(d):
-            if d:
-                b_copy(par, d).wait_recv()
-            target = send_c if d else recv_c
-            for j in range(WCAP):
-                span = slice(j * perf, (j + 1) * perf)
-                live = live_slot[d, :, span]
-                high, low = split_bf16(recv_b[par, d, :, span] * live)
-                left = jnp.where(pick_row == 0, high, jnp.where(pick_row == 1, low, 0.0)).astype(jnp.bfloat16)
-                pushed = jnp.dot(
-                    jnp.concatenate([left, left], 1),
-                    schur_two[d * WCAP + j],
-                    preferred_element_type=jnp.float32,
-                )
-                target[par, d, :, span] = jnp.sum(pushed, axis=0, keepdims=True) * live
-            if d:
-                c_copy(par, d).start()
-
-        for d in range(EARLY):
-            push(d)
+            if group is ranges[0]:
+                start_halos(par)
+
+    def stencil(par):
+        halos = halo_copies(par)
+        x_up, x_down = halos[:2]
+
         @pl.when(me < n - 1)
         def _():
             x_up.wait_send()
@@ -359,9 +364,53 @@
                 + fz_ref[at, :] * (m - pltpu.roll(m, layers - 1, 1))
                 + pz_ref[at, :] * (m - pltpu.roll(m, 1, 1))
             )
-        for d in range(EARLY, n):
-            push(d)
+
+    def push(par):
+        for group in ranges:
+            for d in group:
+                b_copy(par, d).wait_recv()
+            for d in group:
+                for j in range(WCAP):
+                    span = slice(j * perf, (j + 1) * perf)
+                    high, low = split_bf16(recv_b[par, d, :, span])
+                    left = jnp.where(pick_row == 0, high, jnp.where(pick_row == 1, low, 0.0)).astype(
+                        jnp.bfloat16
+                    )
+                    pushed = jnp.dot(
+                        jnp.concatenate([left, left], 1),
+                        schur_two[d * WCAP + j],
+                        preferred_element_type=jnp.float32,
+                    )
+                    send_c[par, d, :, span] = jnp.sum(pushed, axis=0, keepdims=True)
+            for d in group:
+                c_copy(par, d).start()
+
+    def scatter(par, group):
+        for d in group:
+            c_copy(par, d).wait_recv()
+        for d in group:
+            high, low = split_bf16(recv_c[par, d])
+            here = layer == lay_ref[d]
+            span = slice(d * chunk, (d + 1) * chunk)
+            vl_ref[0:layers, span] = jnp.where(here, high, 0.0).astype(jnp.bfloat16)
+            vl_ref[layers : 2 * layers, span] = jnp.where(here, low, 0.0).astype(jnp.bfloat16)
+        span = slice(group[0] * chunk, (group[-1] + 1) * chunk)
+        return lax.dot_general(
+            onehot[:, span],
+            vl_ref[:, span],
+            (((1,), (1,)), ((), ())),
+            preferred_element_type=jnp.float32,
+        )
+
+    def step(k, carried):
+        gam_old, a_old = carried
+        par = lax.rem(k, 2)
+        send_field(par)
+        stencil(par)
+        push(par)
         total = start_sums(par)
+        for d in range(n):
+            b_copy(par, d).wait_send()
         gam, dlt = end_sums(par, total)
         b = jnp.where(k <= 1, 0.0, gam / gam_old)
         a = jnp.where(k == 0, 0.0, jnp.where(k == 1, gam / dlt, gam / (dlt - b * gam / a_old)))
@@ -380,25 +429,12 @@
             r_ref[at, :] = r
             gamma = gamma + jnp.sum((r * r * inverse).reshape(rows_y // 8, 8, layers), axis=0)
 
-        ends = [n * part // 8 for part in GROUPS]
-        for first, end in zip([0] + ends[:-1], ends):
-            for d in range(first, end):
-                if d:
-                    c_copy(par, d).wait_recv()
-                high, low = split_bf16(recv_c[par, d])
-                here = layer == lay_ref[d]
-                span = slice(d * chunk, (d + 1) * chunk)
-                vl_ref[0:layers, span] = jnp.where(here, high, 0.0).astype(jnp.bfloat16)
-                vl_ref[layers : 2 * layers, span] = jnp.where(here, low, 0.0).astype(jnp.bfloat16)
-            span = slice(first * chunk, end * chunk)
-            wide = lax.dot_general(
-                onehot[:, span],
-                vl_ref[:, span],
-                (((1,), (1,)), ((), ())),
-                preferred_element_type=jnp.float32,
-            )
-            if end < n:
-                nloc_ref[...] += wide[:, :layers] + wide[:, layers:]
+        for d in range(n):
+            c_copy(par, d).wait_send()
+        for group in ranges[:0:-1]:
+            wide = scatter(par, group)
+            nloc_ref[...] += wide[:, :layers] + wide[:, layers:]
+        wide = scatter(par, ranges[0])
         delta = jnp.zeros((8, layers), jnp.float32)
         for i in range(rows_x):
             at = slice(i * rows_y, (i + 1) * rows_y)
@@ -414,23 +450,31 @@
         dots_ref[...] = jnp.where(
             first_half, gamma + pltpu.roll(gamma, half, 1), delta + pltpu.roll(delta, half, 1)
         )
-        for d in range(1, n):
-            b_copy(par, d).wait_send()
-            c_copy(par, d).wait_send()
         return gam, a
+
+    for group in ranges:
+        for d in group:
+            swaps[d].wait_recv()
+            for j in range(WCAP):
+                slot = d * WCAP + j
+                block = schur_in[slot]
+                high = block.astype(jnp.bfloat16)
+                schur_two[slot, 0:perf, :] = high
+                schur_two[slot, perf : 2 * perf, :] = (block - high.astype(jnp.float32)).astype(jnp.bfloat16)
+    for copy in swaps:
+        copy.wait_send()
 
     ones = jnp.ones((1, layers), jnp.float32)
     gam_old, a_old = lax.fori_loop(0, ITERS, step, (ones, ones))
 
     par = ITERS % 2
-    recv_b[par, 0, :, chunk:] = dots_ref[...]
-    for d in range(n - 1, 0, -1):
+    for d in range(n - 1, -1, -1):
         send_b[par, d, :, chunk:] = dots_ref[...]
         b_copy(par, d).start()
-    for d in range(1, n):
+    for d in range(n):
         b_copy(par, d).wait_recv()
     total = start_sums(par)
-    for d in range(1, n):
+    for d in range(n):
         b_copy(par, d).wait_send()
     gam, dlt = end_sums(par, total)
     b = gam / gam_old
@@ -481,11 +525,12 @@
         scratch_shapes=[field] * 5
         + [
             vmem((wells, perf, perf), f32),
+            vmem((n * WCAP, perf, perf), f32),
+            vmem((n * WCAP, perf, perf), f32),
             vmem((n * WCAP, 2 * perf, perf), bf16),
             vmem((cols, n * chunk), bf16),
             vmem((2 * layers, n * chunk), bf16),
             vmem((n, 1, chunk), i32),
-            vmem((n, 1, chunk), f32),
             vmem((n, 1, chunk), i32),
             vmem((n, 1, chunk), i32),
             vmem((2, n, 1, chunk + layers), f32),
@@ -507,6 +552,8 @@
             vmem((1, layers), f32),
             dma,
             dma((5,)),
+            dma((n,)),
+            dma((n,)),
             dma((n,)),
             dma((n,)),
             dma((2,)),

time: 92.3 us -> 89 us (0.964)
  Pallas kernels: 91.4 us -> 88.1 us
    pallas_call x1, Pallas kernels: 89.6 us -> 86.2 us  [local(): pl.pallas_call(functools.partial(kernel, n, ny, rows_x, rows_y), out_shap...]
where the time goes in v1:
time: 89 us; the launch traced here: 88.7 us
  Pallas kernels  88.1 us (99%)
    pallas_call x1, Pallas kernels, local(): pl.pallas_call(functools.partial(kernel, n, ny, rows_x, rows_y), out_shap...  86.2 us
    pallas_call x1, Pallas kernels, local(): pl.pallas_call(hand_on, out_shape=[jax.ShapeDtypeStruct((cols, layers), f...  1.84 us

profile of v1, /device:TPU:0, one launch (start us, length us, event | category | flops | bytes accessed | tf_op | source)
XLA Modules:
  0.0 88.7 jit_solution(1561462086113616298)
XLA Ops:
  0.6 86.2 %shard_map.104 = (f32[512,128]{1,0:T(8,128)}, f32[512,128]{1,0:T(8,128)}) custom-call(s32[1,16]{1,0:T(1,128)} %bitcast.13, f32[512,128]{1,0:T(8,128)} %bitcast.8, f32[512,128]{1,0:T(8,128)} %bitcast.9, f32[512,128]{1,0:T(8,128)} %bitcast.10, f32[512,128]{1,0:T(8,128)} %bitcast.11, f32[512,128]{1,0:T(8,128)} %bitcast.12, s32[16,256]{1,0:T(8,128)} %cells_ref.1, ...), custom_call_target="tpu_custom_call" | custom-call | tf_op jit(solution)/shard_map/pallas_call | solution.py:517
  86.9 1.8 %shard_map.105 = (f32[512,128]{1,0:T(8,128)}, f32[512,128]{1,0:T(8,128)}) custom-call(f32[512,128]{1,0:T(8,128)} %get-tuple-element.6.x_ref, f32[512,128]{1,0:T(8,128)} %get-tuple-element.7.r_ref), custom_call_target="tpu_custom_call" | custom-call | tf_op jit(solution)/shard_map/pallas_call | solution.py:574

commit v2 on v1

--- a/solution.py
+++ b/solution.py
@@ -9,6 +9,9 @@
 
 WCAP = 2
 ITERS = 6
+SEND = ((7, 8), (1, 3), (3, 5), (5, 7), (0, 1))
+PUSH = ((0, 1), (1, 3), (7, 8), (3, 5), (5, 7))
+SCATTER = ((0, 3), (3, 5), (5, 8))
 MESH = pl.DeviceIdType.MESH
 
 
@@ -72,6 +75,9 @@
     s_ref,
     nloc_ref,
     dots_ref,
+    last_send,
+    last_recv,
+    well_dot,
     local_sem,
     field_sem,
     schur_ss,
@@ -88,6 +94,8 @@
     c_rs,
     g_ss,
     g_rs,
+    last_ss,
+    last_rs,
 ):
     cols, layers = rhs_ref.shape
     wells, perf = cells_ref.shape
@@ -141,12 +149,9 @@
     schur_copy.start()
     xrecv[...] = jnp.zeros_like(xrecv)
     barrier = pltpu.get_barrier_semaphore()
-    for d in range(1, n):
-        pl.semaphore_signal(barrier, inc=1, device_id=at_peer(d), device_id_type=MESH)
-    for d in range(1, ny):
-        pl.semaphore_signal(barrier, inc=1, device_id=at_y(d), device_id_type=MESH)
-    for d in range(1, n):
-        pl.semaphore_signal(barrier, inc=1, device_id=at_cross(d), device_id_type=MESH)
+    others = [(d, e) for d in range(n - 1, -1, -1) for e in range(ny) if d or e]
+    for d, e in others:
+        pl.semaphore_signal(barrier, inc=1, device_id={"gx": across(d), **at_y(e)}, device_id_type=MESH)
 
     well_at = []
     for d in range(n):
@@ -169,7 +174,7 @@
     loads[1].wait()
     yface_send[...] = ty_ref[pl.ds(rows_y - 1, rows_x, stride=rows_y), :]
 
-    pl.semaphore_wait(barrier, 2 * (n - 1) + ny - 1)
+    pl.semaphore_wait(barrier, len(others))
     requests = [
         remote(req_send.at[d], req_recv.at[d], req_ss.at[d], req_rs.at[d], at_peer(d)) for d in range(1, n)
     ]
@@ -182,11 +187,10 @@
     for copy in requests[::-1] + face_out:
         copy.start()
 
-    edges = [n, n - 1]
-    while edges[-1] > 3:
-        edges.append(edges[-1] - 2)
-    edges.append(0)
-    ranges = [range(low, high) for high, low in zip(edges[:-1], edges[1:])]
+    def cut(parts):
+        return [range(n * low // 8, n * high // 8) for low, high in parts]
+
+    sends, pushes, scatters = cut(SEND), cut(PUSH), cut(SCATTER)
     swaps = [
         remote(
             schur_out.at[pl.ds(d * WCAP, WCAP)],
@@ -198,7 +202,7 @@
         for d in range(n)
     ]
     schur_copy.wait()
-    for group in ranges:
+    for group in pushes:
         for d in group:
             for j in range(WCAP):
                 schur_out[d * WCAP + j] = schur_vm[well_at[d][j]]
@@ -317,7 +321,7 @@
         high, low = split_bf16(m_ref[...].T)
         lhs = jnp.concatenate([high, low], 0).astype(jnp.bfloat16)
         dots = dots_ref[...]
-        for group in ranges:
+        for group in sends:
             for d in group:
                 part = jnp.dot(
                     lhs, onehot[:, d * chunk : (d + 1) * chunk], preferred_element_type=jnp.float32
@@ -328,7 +332,7 @@
                 send_b[par, d, :, chunk:] = dots
             for d in group:
                 b_copy(par, d).start()
-            if group is ranges[0]:
+            if group is sends[0]:
                 start_halos(par)
 
     def stencil(par):
@@ -365,8 +369,8 @@
                 + pz_ref[at, :] * (m - pltpu.roll(m, 1, 1))
             )
 
-    def push(par):
-        for group in ranges:
+    def push(par, keep=False):
+        for group in pushes:
             for d in group:
                 b_copy(par, d).wait_recv()
             for d in group:
@@ -381,7 +385,12 @@
                         schur_two[d * WCAP + j],
                         preferred_element_type=jnp.float32,
                     )
-                    send_c[par, d, :, span] = jnp.sum(pushed, axis=0, keepdims=True)
+                    pushed = jnp.sum(pushed, axis=0, keepdims=True)
+                    send_c[par, d, :, span] = pushed
+                    if keep:
+                        part = recv_b[par, d, :, span] * pushed
+                        for low_lane in range(0, perf, layers):
+                            well_dot[...] += part[:, low_lane : low_lane + layers]
             for d in group:
                 c_copy(par, d).start()
 
@@ -402,19 +411,7 @@
             preferred_element_type=jnp.float32,
         )
 
-    def step(k, carried):
-        gam_old, a_old = carried
-        par = lax.rem(k, 2)
-        send_field(par)
-        stencil(par)
-        push(par)
-        total = start_sums(par)
-        for d in range(n):
-            b_copy(par, d).wait_send()
-        gam, dlt = end_sums(par, total)
-        b = jnp.where(k <= 1, 0.0, gam / gam_old)
-        a = jnp.where(k == 0, 0.0, jnp.where(k == 1, gam / dlt, gam / (dlt - b * gam / a_old)))
-        a_w = jnp.where(k == 0, -1.0, a)
+    def advance(a, b):
         gamma = jnp.zeros((8, layers), jnp.float32)
         for i in range(rows_x):
             at = slice(i * rows_y, (i + 1) * rows_y)
@@ -428,13 +425,36 @@
             r = r - a * s
             r_ref[at, :] = r
             gamma = gamma + jnp.sum((r * r * inverse).reshape(rows_y // 8, 8, layers), axis=0)
-
-        for d in range(n):
-            c_copy(par, d).wait_send()
-        for group in ranges[:0:-1]:
+        return gamma
+
+    def tiles(values):
+        return jnp.sum(values.reshape(rows_y // 8, 8, layers), axis=0)
+
+    def last_copy(d, e):
+        slot = d * ny + (ny - e) % ny
+        return remote(
+            last_send, last_recv.at[slot], last_ss, last_rs, {"gx": across(d), **at_y(e)}
+        )
+
+    def step(k, carried):
+        gam_old, a_old = carried
+        par = lax.rem(k, 2)
+        send_field(par)
+        push(par)
+        total = start_sums(par)
+        stencil(par)
+        for group in scatters[:-1]:
             wide = scatter(par, group)
             nloc_ref[...] += wide[:, :layers] + wide[:, layers:]
-        wide = scatter(par, ranges[0])
+        for d in range(n):
+            b_copy(par, d).wait_send()
+            c_copy(par, d).wait_send()
+        gam, dlt = end_sums(par, total)
+        b = jnp.where(k <= 1, 0.0, gam / gam_old)
+        a = jnp.where(k == 0, 0.0, jnp.where(k == 1, gam / dlt, gam / (dlt - b * gam / a_old)))
+        a_w = jnp.where(k == 0, -1.0, a)
+        gamma = advance(a, b)
+        wide = scatter(par, scatters[-1])
         delta = jnp.zeros((8, layers), jnp.float32)
         for i in range(rows_x):
             at = slice(i * rows_y, (i + 1) * rows_y)
@@ -452,7 +472,7 @@
         )
         return gam, a
 
-    for group in ranges:
+    for group in pushes:
         for d in group:
             swaps[d].wait_recv()
             for j in range(WCAP):
@@ -465,27 +485,77 @@
         copy.wait_send()
 
     ones = jnp.ones((1, layers), jnp.float32)
-    gam_old, a_old = lax.fori_loop(0, ITERS, step, (ones, ones))
-
-    par = ITERS % 2
-    for d in range(n - 1, -1, -1):
-        send_b[par, d, :, chunk:] = dots_ref[...]
-        b_copy(par, d).start()
-    for d in range(n):
-        b_copy(par, d).wait_recv()
+    gam_old, a_old = lax.fori_loop(0, ITERS - 1, step, (ones, ones))
+
+    par = (ITERS - 1) % 2
+    send_field(par)
+    zero = jnp.zeros((8, layers), jnp.float32)
+    sums = [zero] * 6
+    for i in range(rows_x):
+        at = slice(i * rows_y, (i + 1) * rows_y)
+        inverse, w, s, z, m = inv_ref[at, :], w_ref[at, :], s_ref[at, :], z_ref[at, :], m_ref[at, :]
+        q = s * inverse
+        terms = (w * m, q * r_ref[at, :], s * m, s * q, z * m, z * q)
+        sums = [total + tiles(term) for total, term in zip(sums, terms)]
+    well_dot[...] = jnp.zeros_like(well_dot)
+    push(par, keep=True)
     total = start_sums(par)
+    stencil(par)
+    image_dot = zero
+    for i in range(rows_x):
+        at = slice(i * rows_y, (i + 1) * rows_y)
+        image_dot = image_dot + tiles(m_ref[at, :] * nloc_ref[at, :])
+    rows = [jnp.sum(value, axis=0, keepdims=True) for value in sums + [image_dot]]
+    rows[-1] = rows[-1] + well_dot[...]
+    values = len(rows) + 1
+    width = layers // values
+    lane_row = lax.broadcasted_iota(jnp.int32, (1, layers), 1)
+    packed = jnp.zeros((1, layers), jnp.float32)
+    for index, value in enumerate(rows):
+        fold = half
+        while fold >= width:
+            value = value + pltpu.roll(value, fold, 1)
+            fold //= 2
+        packed = jnp.where(lane_row // width == index, value, packed)
+    last_send[...] = packed
+    for d, e in others:
+        last_copy(d, e).start()
+    for group in scatters[:-1]:
+        wide = scatter(par, group)
+        nloc_ref[...] += wide[:, :layers] + wide[:, layers:]
     for d in range(n):
         b_copy(par, d).wait_send()
+        c_copy(par, d).wait_send()
     gam, dlt = end_sums(par, total)
     b = gam / gam_old
     a = gam / (dlt - b * gam / a_old)
+    advance(a, b)
+    wide = scatter(par, scatters[-1])
+    arrived = last_recv.at[pl.ds(1, len(others))]
+    pltpu.make_async_copy(arrived, arrived, last_rs).wait()
+    pltpu.make_async_copy(arrived, arrived, last_ss).wait()
+    packed = last_send[...]
+    for slot in range(1, len(others) + 1):
+        packed = packed + last_recv[slot]
+
+    def value_of(index):
+        value = jnp.sum(jnp.where(lane_row // width == index, packed, 0.0), axis=1, keepdims=True)
+        return jnp.broadcast_to(value, (1, layers))
+
+    wm, su, sm, sq, zm, zq, am = [value_of(index) for index in range(len(rows))]
+    gam_new = gam - 2.0 * a * (dlt + b * su) + a * a * (wm + 2.0 * b * sm + b * b * sq)
+    dlt_new = dlt - 2.0 * a * (wm + b * sm) + a * a * (am + 2.0 * b * zm + b * b * zq)
+    b_new = gam_new / gam
+    a_new = gam_new / (dlt_new - b_new * gam_new / a)
     for i in range(rows_x):
         at = slice(i * rows_y, (i + 1) * rows_y)
+        z = nloc_ref[at, :] + (wide[at, :layers] + wide[at, layers:]) + b * z_ref[at, :]
+        w = w_ref[at, :] - a * z
         r = r_ref[at, :]
-        p = r * inv_ref[at, :] + b * p_ref[at, :]
-        s = w_ref[at, :] + b * s_ref[at, :]
-        x_ref[at, :] = x_ref[at, :] + a * p
-        r_ref[at, :] = r - a * s
+        p = r * inv_ref[at, :] + b_new * p_ref[at, :]
+        s = w + b_new * s_ref[at, :]
+        x_ref[at, :] = x_ref[at, :] + a_new * p
+        r_ref[at, :] = r - a_new * s
 
 
 def hand_on(x_ref, r_ref, x_out, r_out):
@@ -550,6 +620,9 @@
         + [field] * 11
         + [
             vmem((1, layers), f32),
+            vmem((1, layers), f32),
+            vmem((n * ny, 1, layers), f32),
+            vmem((1, layers), f32),
             dma,
             dma((5,)),
             dma((n,)),
@@ -566,6 +639,8 @@
             dma((2, n)),
             dma((2, ny)),
             dma((2, ny)),
+            dma,
+            dma,
         ],
         compiler_params=pltpu.CompilerParams(
             collective_id=0, has_side_effects=True, vmem_limit_bytes=60 * 1024 * 1024

time: 89 us -> 75.3 us (0.85)
  Pallas kernels: 88.1 us -> 74.4 us
    pallas_call x1, Pallas kernels: 86.2 us -> 72.6 us  [local(): pl.pallas_call(functools.partial(kernel, n, ny, rows_x, rows_y), out_shap...]
where the time goes in v2:
time: 75.3 us; the launch traced here: 75.1 us
  Pallas kernels  74.4 us (99%)
    pallas_call x1, Pallas kernels, local(): pl.pallas_call(functools.partial(kernel, n, ny, rows_x, rows_y), out_shap...  72.6 us
    pallas_call x1, Pallas kernels, local(): pl.pallas_call(hand_on, out_shape=[jax.ShapeDtypeStruct((cols, layers), f...  1.84 us

profile of v2, /device:TPU:0, one launch (start us, length us, event | category | flops | bytes accessed | tf_op | source)
XLA Modules:
  0.0 75.1 jit_solution(15286559837014703540)
XLA Ops:
  0.6 72.6 %shard_map.104 = (f32[512,128]{1,0:T(8,128)}, f32[512,128]{1,0:T(8,128)}) custom-call(s32[1,16]{1,0:T(1,128)} %bitcast.13, f32[512,128]{1,0:T(8,128)} %bitcast.8, f32[512,128]{1,0:T(8,128)} %bitcast.9, f32[512,128]{1,0:T(8,128)} %bitcast.10, f32[512,128]{1,0:T(8,128)} %bitcast.11, f32[512,128]{1,0:T(8,128)} %bitcast.12, s32[16,256]{1,0:T(8,128)} %cells_ref.1, ...), custom_call_target="tpu_custom_call" | custom-call | tf_op jit(solution)/shard_map/pallas_call | solution.py:587
  73.2 1.8 %shard_map.105 = (f32[512,128]{1,0:T(8,128)}, f32[512,128]{1,0:T(8,128)}) custom-call(f32[512,128]{1,0:T(8,128)} %get-tuple-element.6.x_ref, f32[512,128]{1,0:T(8,128)} %get-tuple-element.7.r_ref), custom_call_target="tpu_custom_call" | custom-call | tf_op jit(solution)/shard_map/pallas_call | solution.py:649

commit v3 on v2

--- a/solution.py
+++ b/solution.py
@@ -25,17 +25,20 @@
     ny,
     rows_x,
     rows_y,
-    region_ref,
+    region_hbm,
     rhs_hbm,
     acc_hbm,
     tx_hbm,
     ty_hbm,
     tz_hbm,
-    cells_ref,
-    live_ref,
+    cells_hbm,
+    live_hbm,
     schur_hbm,
     x_ref,
     r_ref,
+    region_ref,
+    cells_ref,
+    live_ref,
     rhs_ref,
     acc_ref,
     tx_ref,
@@ -80,6 +83,7 @@
     well_dot,
     local_sem,
     field_sem,
+    small_sem,
     schur_ss,
     schur_rs,
     req_ss,
@@ -144,14 +148,25 @@
             )
         )
     ]
+    small = [
+        pltpu.make_async_copy(src, dst, small_sem.at[i])
+        for i, (src, dst) in enumerate(
+            ((region_hbm, region_ref), (cells_hbm, cells_ref), (live_hbm, live_ref))
+        )
+    ]
+    for copy in small:
+        copy.start()
+    barrier = pltpu.get_barrier_semaphore()
+    others = [(d, e) for d in range(n - 1, -1, -1) for e in range(ny) if d or e]
+    for d, e in others:
+        pl.semaphore_signal(barrier, inc=1, device_id={"gx": across(d), **at_y(e)}, device_id_type=MESH)
+
     for copy in loads:
         copy.start()
     schur_copy.start()
     xrecv[...] = jnp.zeros_like(xrecv)
-    barrier = pltpu.get_barrier_semaphore()
-    others = [(d, e) for d in range(n - 1, -1, -1) for e in range(ny) if d or e]
-    for d, e in others:
-        pl.semaphore_signal(barrier, inc=1, device_id={"gx": across(d), **at_y(e)}, device_id_type=MESH)
+    for copy in small:
+        copy.wait()
 
     well_at = []
     for d in range(n):
@@ -213,6 +228,19 @@
     lane = lax.broadcasted_iota(jnp.int32, (rows_y, layers), 1)
     row = lax.broadcasted_iota(jnp.int32, (rows_y, layers), 0)
     zeros = jnp.zeros((rows_y, layers), jnp.float32)
+    column = lax.broadcasted_iota(jnp.int32, (cols, chunk), 0)
+
+    def mark_slots(group):
+        for d in group:
+            if d:
+                requests[d - 1].wait_recv()
+            cells = req_recv[d]
+            lay_ref[d] = jnp.bitwise_and(cells, layers - 1)
+            onehot[:, d * chunk : (d + 1) * chunk] = (
+                (column == lax.shift_right_logical(cells, shift)).astype(jnp.float32).astype(jnp.bfloat16)
+            )
+
+    mark_slots(range(n * 5 // 8))
     for copy in loads[2:]:
         copy.wait()
     for copy in face_out:
@@ -246,15 +274,7 @@
             ref[at, :] = zeros
     dots_ref[...] = jnp.zeros_like(dots_ref)
 
-    column = lax.broadcasted_iota(jnp.int32, (cols, chunk), 0)
-    for d in range(n):
-        if d:
-            requests[d - 1].wait_recv()
-        cells = req_recv[d]
-        lay_ref[d] = jnp.bitwise_and(cells, layers - 1)
-        onehot[:, d * chunk : (d + 1) * chunk] = (
-            (column == lax.shift_right_logical(cells, shift)).astype(jnp.float32).astype(jnp.bfloat16)
-        )
+    mark_slots(range(n * 5 // 8, n))
     for copy in requests:
         copy.wait_send()
 
@@ -439,7 +459,6 @@
     def step(k, carried):
         gam_old, a_old = carried
         par = lax.rem(k, 2)
-        send_field(par)
         push(par)
         total = start_sums(par)
         stencil(par)
@@ -470,8 +489,10 @@
         dots_ref[...] = jnp.where(
             first_half, gamma + pltpu.roll(gamma, half, 1), delta + pltpu.roll(delta, half, 1)
         )
+        send_field(lax.rem(k + 1, 2))
         return gam, a
 
+    send_field(0)
     for group in pushes:
         for d in group:
             swaps[d].wait_recv()
@@ -488,7 +509,6 @@
     gam_old, a_old = lax.fori_loop(0, ITERS - 1, step, (ones, ones))
 
     par = (ITERS - 1) % 2
-    send_field(par)
     zero = jnp.zeros((8, layers), jnp.float32)
     sums = [zero] * 6
     for i in range(rows_x):
@@ -587,12 +607,14 @@
     outs = pl.pallas_call(
         functools.partial(kernel, n, ny, rows_x, rows_y),
         out_shape=[jax.ShapeDtypeStruct((cols, layers), f32)] * 2,
-        in_specs=[pl.BlockSpec(memory_space=pltpu.SMEM)]
-        + [pl.BlockSpec(memory_space=pl.ANY)] * 5
-        + [in_vmem] * 2
-        + [pl.BlockSpec(memory_space=pl.ANY)],
+        in_specs=[pl.BlockSpec(memory_space=pl.ANY)] * 9,
         out_specs=[in_vmem] * 2,
-        scratch_shapes=[field] * 5
+        scratch_shapes=[
+            pltpu.SMEM((1, wells), i32),
+            vmem((wells, perf), i32),
+            vmem((wells, perf), i32),
+        ]
+        + [field] * 5
         + [
             vmem((wells, perf, perf), f32),
             vmem((n * WCAP, perf, perf), f32),
@@ -625,6 +647,7 @@
             vmem((1, layers), f32),
             dma,
             dma((5,)),
+            dma((3,)),
             dma((n,)),
             dma((n,)),
             dma((n,)),

time: 75.3 us -> 71.8 us (0.954)
  Pallas kernels: 74.4 us -> 71 us
    pallas_call x1, Pallas kernels: 72.6 us -> 69.2 us  [local(): pl.pallas_call(functools.partial(kernel, n, ny, rows_x, rows_y), out_shap...]
where the time goes in v3:
time: 71.8 us; the launch traced here: 71.7 us
  Pallas kernels  71 us (99%)
    pallas_call x1, Pallas kernels, local(): pl.pallas_call(functools.partial(kernel, n, ny, rows_x, rows_y), out_shap...  69.2 us
    pallas_call x1, Pallas kernels, local(): pl.pallas_call(hand_on, out_shape=[jax.ShapeDtypeStruct((cols, layers), f...  1.84 us

profile of v3, /device:TPU:0, one launch (start us, length us, event | category | flops | bytes accessed | tf_op | source)
XLA Modules:
  0.0 71.7 jit_solution(2061464939122098180)
XLA Ops:
  0.6 69.2 %shard_map.104 = (f32[512,128]{1,0:T(8,128)}, f32[512,128]{1,0:T(8,128)}) custom-call(s32[1,16]{1,0:T(1,128)} %bitcast.13, f32[512,128]{1,0:T(8,128)} %bitcast.8, f32[512,128]{1,0:T(8,128)} %bitcast.9, f32[512,128]{1,0:T(8,128)} %bitcast.10, f32[512,128]{1,0:T(8,128)} %bitcast.11, f32[512,128]{1,0:T(8,128)} %bitcast.12, s32[16,256]{1,0:T(8,128)} %cells_hbm.1, ...), custom_call_target="tpu_custom_call" | custom-call | tf_op jit(solution)/shard_map/pallas_call | solution.py:607
  69.9 1.8 %shard_map.105 = (f32[512,128]{1,0:T(8,128)}, f32[512,128]{1,0:T(8,128)}) custom-call(f32[512,128]{1,0:T(8,128)} %get-tuple-element.6.x_ref, f32[512,128]{1,0:T(8,128)} %get-tuple-element.7.r_ref), custom_call_target="tpu_custom_call" | custom-call | tf_op jit(solution)/shard_map/pallas_call | solution.py:672

commit v4 on v3

--- a/solution.py
+++ b/solution.py
@@ -9,7 +9,9 @@
 
 WCAP = 2
 ITERS = 6
+NEAR = 1
 SEND = ((7, 8), (1, 3), (3, 5), (5, 7), (0, 1))
+GAP = 2
 PUSH = ((0, 1), (1, 3), (7, 8), (3, 5), (5, 7))
 SCATTER = ((0, 3), (3, 5), (5, 8))
 MESH = pl.DeviceIdType.MESH
@@ -130,6 +132,11 @@
     def at_cross(d):
         return {"gx": across(d), **at_other()}
 
+    near = n * NEAR // 8
+
+    def at_pair(d):
+        return at_peer(d) if d < near else at_cross(d)
+
     def remote(src, dst, ss, rs, where):
         return pltpu.make_async_remote_copy(
             src_ref=src, dst_ref=dst, send_sem=ss, recv_sem=rs, device_id=where, device_id_type=MESH
@@ -214,14 +221,15 @@
             schur_rs.at[d],
             at_other(),
         )
-        for d in range(n)
+        for d in range(near, n)
     ]
     schur_copy.wait()
     for group in pushes:
         for d in group:
-            for j in range(WCAP):
-                schur_out[d * WCAP + j] = schur_vm[well_at[d][j]]
-            swaps[d].start()
+            if d >= near:
+                for j in range(WCAP):
+                    schur_out[d * WCAP + j] = schur_vm[well_at[d][j]]
+                swaps[d - near].start()
 
     last_x = me == n - 1
     last_y = my == ny - 1
@@ -285,10 +293,10 @@
     first_half = lax.broadcasted_iota(jnp.int32, (1, layers), 1) < half
 
     def b_copy(par, d):
-        return remote(send_b.at[par, d], recv_b.at[par, d], b_ss.at[par, d], b_rs.at[par, d], at_cross(d))
+        return remote(send_b.at[par, d], recv_b.at[par, d], b_ss.at[par, d], b_rs.at[par, d], at_pair(d))
 
     def c_copy(par, d):
-        return remote(send_c.at[par, d], recv_c.at[par, d], c_ss.at[par, d], c_rs.at[par, d], at_cross(d))
+        return remote(send_c.at[par, d], recv_c.at[par, d], c_ss.at[par, d], c_rs.at[par, d], at_pair(d))
 
     def g_copy(par, d, slot):
         return remote(send_g.at[par], recv_g.at[par, slot], g_ss.at[par, d], g_rs.at[par, slot], at_y(d))
@@ -348,10 +356,12 @@
                 )
                 part = part[:layers] + part[layers:]
                 picked = jnp.sum(jnp.where(layer == lay_ref[d], part, 0.0), axis=0, keepdims=True)
-                send_b[par, d, :, :chunk] = picked
-                send_b[par, d, :, chunk:] = dots
+                target = send_b if d else recv_b
+                target[par, d, :, :chunk] = picked
+                target[par, d, :, chunk:] = dots
             for d in group:
-                b_copy(par, d).start()
+                if d:
+                    b_copy(par, d).start()
             if group is sends[0]:
                 start_halos(par)
 
@@ -389,11 +399,15 @@
                 + pz_ref[at, :] * (m - pltpu.roll(m, 1, 1))
             )
 
-    def push(par, keep=False):
-        for group in pushes:
+    def push(par, keep=False, between=None):
+        for index, group in enumerate(pushes):
+            if between and index == GAP:
+                between()
             for d in group:
-                b_copy(par, d).wait_recv()
+                if d:
+                    b_copy(par, d).wait_recv()
             for d in group:
+                target = send_c if d else recv_c
                 for j in range(WCAP):
                     span = slice(j * perf, (j + 1) * perf)
                     high, low = split_bf16(recv_b[par, d, :, span])
@@ -406,17 +420,19 @@
                         preferred_element_type=jnp.float32,
                     )
                     pushed = jnp.sum(pushed, axis=0, keepdims=True)
-                    send_c[par, d, :, span] = pushed
+                    target[par, d, :, span] = pushed
                     if keep:
                         part = recv_b[par, d, :, span] * pushed
                         for low_lane in range(0, perf, layers):
                             well_dot[...] += part[:, low_lane : low_lane + layers]
             for d in group:
-                c_copy(par, d).start()
+                if d:
+                    c_copy(par, d).start()
 
     def scatter(par, group):
         for d in group:
-            c_copy(par, d).wait_recv()
+            if d:
+                c_copy(par, d).wait_recv()
         for d in group:
             high, low = split_bf16(recv_c[par, d])
             here = layer == lay_ref[d]
@@ -465,7 +481,7 @@
         for group in scatters[:-1]:
             wide = scatter(par, group)
             nloc_ref[...] += wide[:, :layers] + wide[:, layers:]
-        for d in range(n):
+        for d in range(1, n):
             b_copy(par, d).wait_send()
             c_copy(par, d).wait_send()
         gam, dlt = end_sums(par, total)
@@ -495,10 +511,11 @@
     send_field(0)
     for group in pushes:
         for d in group:
-            swaps[d].wait_recv()
+            if d >= near:
+                swaps[d - near].wait_recv()
             for j in range(WCAP):
                 slot = d * WCAP + j
-                block = schur_in[slot]
+                block = schur_in[slot] if d >= near else schur_vm[well_at[d][j]]
                 high = block.astype(jnp.bfloat16)
                 schur_two[slot, 0:perf, :] = high
                 schur_two[slot, perf : 2 * perf, :] = (block - high.astype(jnp.float32)).astype(jnp.bfloat16)
@@ -518,9 +535,7 @@
         terms = (w * m, q * r_ref[at, :], s * m, s * q, z * m, z * q)
         sums = [total + tiles(term) for total, term in zip(sums, terms)]
     well_dot[...] = jnp.zeros_like(well_dot)
-    push(par, keep=True)
-    total = start_sums(par)
-    stencil(par)
+    push(par, keep=True, between=lambda: stencil(par))
     image_dot = zero
     for i in range(rows_x):
         at = slice(i * rows_y, (i + 1) * rows_y)
@@ -540,10 +555,11 @@
     last_send[...] = packed
     for d, e in others:
         last_copy(d, e).start()
+    total = start_sums(par)
     for group in scatters[:-1]:
         wide = scatter(par, group)
         nloc_ref[...] += wide[:, :layers] + wide[:, layers:]
-    for d in range(n):
+    for d in range(1, n):
         b_copy(par, d).wait_send()
         c_copy(par, d).wait_send()
     gam, dlt = end_sums(par, total)

time: 71.8 us -> 71.6 us (level)
  no operation moved by 1% of the time
where the time goes in v4:
time: 71.6 us; the launch traced here: 71.4 us
  Pallas kernels  70.8 us (99%)
    pallas_call x1, Pallas kernels, local(): pl.pallas_call(functools.partial(kernel, n, ny, rows_x, rows_y), out_shap...  69 us
    pallas_call x1, Pallas kernels, local(): pl.pallas_call(hand_on, out_shape=[jax.ShapeDtypeStruct((cols, layers), f...  1.84 us

profile of v4, /device:TPU:0, one launch (start us, length us, event | category | flops | bytes accessed | tf_op | source)
XLA Modules:
  0.0 71.4 jit_solution(69010439937802568)
XLA Ops:
  0.6 69.0 %shard_map.104 = (f32[512,128]{1,0:T(8,128)}, f32[512,128]{1,0:T(8,128)}) custom-call(s32[1,16]{1,0:T(1,128)} %bitcast.13, f32[512,128]{1,0:T(8,128)} %bitcast.8, f32[512,128]{1,0:T(8,128)} %bitcast.9, f32[512,128]{1,0:T(8,128)} %bitcast.10, f32[512,128]{1,0:T(8,128)} %bitcast.11, f32[512,128]{1,0:T(8,128)} %bitcast.12, s32[16,256]{1,0:T(8,128)} %cells_hbm.1, ...), custom_call_target="tpu_custom_call" | custom-call | tf_op jit(solution)/shard_map/pallas_call | solution.py:623
  69.6 1.8 %shard_map.105 = (f32[512,128]{1,0:T(8,128)}, f32[512,128]{1,0:T(8,128)}) custom-call(f32[512,128]{1,0:T(8,128)} %get-tuple-element.6.x_ref, f32[512,128]{1,0:T(8,128)} %get-tuple-element.7.r_ref), custom_call_target="tpu_custom_call" | custom-call | tf_op jit(solution)/shard_map/pallas_call | solution.py:688

commit v5 on v4

--- a/solution.py
+++ b/solution.py
@@ -13,7 +13,7 @@
 SEND = ((7, 8), (1, 3), (3, 5), (5, 7), (0, 1))
 GAP = 2
 PUSH = ((0, 1), (1, 3), (7, 8), (3, 5), (5, 7))
-SCATTER = ((0, 3), (3, 5), (5, 8))
+SCATTER = ((0, 1), (1, 3), (3, 5), (5, 8))
 MESH = pl.DeviceIdType.MESH
 
 

time: 71.6 us -> 71.6 us (level)
  no operation moved by 1% of the time
where the time goes in v5:
time: 71.6 us; the launch traced here: 71.4 us
  Pallas kernels  70.8 us (99%)
    pallas_call x1, Pallas kernels, local(): pl.pallas_call(functools.partial(kernel, n, ny, rows_x, rows_y), out_shap...  69 us
    pallas_call x1, Pallas kernels, local(): pl.pallas_call(hand_on, out_shape=[jax.ShapeDtypeStruct((cols, layers), f...  1.84 us

profile of v5, /device:TPU:0, one launch (start us, length us, event | category | flops | bytes accessed | tf_op | source)
XLA Modules:
  0.0 71.4 jit_solution(2410759096949666937)
XLA Ops:
  0.6 69.0 %shard_map.104 = (f32[512,128]{1,0:T(8,128)}, f32[512,128]{1,0:T(8,128)}) custom-call(s32[1,16]{1,0:T(1,128)} %bitcast.13, f32[512,128]{1,0:T(8,128)} %bitcast.8, f32[512,128]{1,0:T(8,128)} %bitcast.9, f32[512,128]{1,0:T(8,128)} %bitcast.10, f32[512,128]{1,0:T(8,128)} %bitcast.11, f32[512,128]{1,0:T(8,128)} %bitcast.12, s32[16,256]{1,0:T(8,128)} %cells_hbm.1, ...), custom_call_target="tpu_custom_call" | custom-call | tf_op jit(solution)/shard_map/pallas_call | solution.py:623
  69.6 1.8 %shard_map.105 = (f32[512,128]{1,0:T(8,128)}, f32[512,128]{1,0:T(8,128)}) custom-call(f32[512,128]{1,0:T(8,128)} %get-tuple-element.6.x_ref, f32[512,128]{1,0:T(8,128)} %get-tuple-element.7.r_ref), custom_call_target="tpu_custom_call" | custom-call | tf_op jit(solution)/shard_map/pallas_call | solution.py:688
